TPU v7x, 32 devices: a whole 2x2x4 slice. The times are simulated.
32 devices in a mesh: frames: 4 (over x, core), feat: 8 (over z, y).
Axes of the slice: x: 2, y: 2, z: 4, core: 2. Of those that a mesh axis runs over, the one named last changes fastest.
Arguments:
- acoustic: float32 [1024, 440], P('frames'), may hold values from -6 to 6
- projection: float32 [440, 8192], P(None, 'feat'), may hold values from -0.25 to 0.25
- phases: float32 [8192], P('feat'), may hold values from -3.140625 to 3.140625
- labels: int32 [1024], P('frames'), may hold values from 0 to 146
- weights: float32 [147, 8192], P(None, 'feat'), may hold values from -1.5 to 1.5
- scaled_duals: float32 [147, 1024], P(None, 'frames'), may hold values from -7 to 7
Outputs:
- weights_out: float32 [147, 8192], P(None, 'feat')
- duals_out: float32 [147, 1024], P(None, ('frames', 'feat'))
- penalty: float32 [], replicated
All inputs are finite; a program needn't handle non-finite values.
Results may differ from a plain program's by a relative error of at most 0.0003.
Values sent between devices are 32-bit elements; how exact they have to be, the bound alone decides.
No kernel may reach another device: no remote copies, remote signals or barrier semaphores. Data moves between devices by JAX's collectives and lax.ppermute only.
A program may use at most 64 MiB of HBM per device.

v0:
```python
import jax
import jax.numpy as jnp
from jax import lax
from jax.sharding import PartitionSpec as P

ITERS = 2
highest = lax.Precision.HIGHEST
epsilon = 1e-06
ridge_weight = 2.0


def cosine_features(acoustic, projection, phases, total_features):
    mixed = (
        jnp.dot(acoustic, projection, precision=highest, preferred_element_type=jnp.float32)
        + phases[None, :]
    )
    return jnp.sqrt(2.0 / total_features) * jnp.cos(mixed)


def ridge_solve(factor, right):
    middle = lax.linalg.triangular_solve(
        factor, right, left_side=False, lower=True, transpose_a=True
    )
    return lax.linalg.triangular_solve(
        factor, middle, left_side=False, lower=True, transpose_a=False
    )


def proximal(predicted, duals, target, penalty):
    shifted = predicted + duals
    inner = (2.0 * target + penalty * shifted) / (2.0 + penalty)
    split = jnp.where(target * shifted < 1.0, inner, shifted)
    miss = predicted - split
    duals_next = duals + miss
    residual = split - duals_next - predicted
    return (miss, duals_next, residual)


def shards(acoustic, projection, phases, labels, weights, scaled_duals):
    frames_here = acoustic.shape[0]
    block_width = projection.shape[1]
    class_count = weights.shape[0]
    feat_count = lax.axis_size("feat")
    group_count = lax.axis_size("frames")
    total_features = block_width * feat_count
    total_frames = frames_here * group_count
    ridge = frames_here / total_features
    share = frames_here // feat_count
    offset = lax.axis_index("feat") * share
    basis = cosine_features(acoustic, projection, phases, total_features)
    inner_matrix = ridge * jnp.eye(frames_here, dtype=jnp.float32) + lax.dot_general(
        basis, basis, (((1,), (1,)), ((), ())), precision=highest
    )
    factor = jnp.linalg.cholesky(inner_matrix)
    classes = lax.broadcasted_iota(jnp.int32, (class_count, frames_here), 0)
    target = jnp.where(classes == labels[None, :], 1.0, -1.0).astype(jnp.float32)
    duals = scaled_duals
    penalty = jnp.ones((), jnp.float32)
    for iteration in range(ITERS):
        partial_value = lax.dot_general(weights, basis, (((1,), (1,)), ((), ())), precision=highest)
        predicted = lax.psum(partial_value, "feat")
        miss, duals, residual = proximal(predicted, duals, target, penalty)
        mine = lax.dynamic_slice_in_dim(miss, offset, share, 1)
        primal_part = jnp.sum(mine * mine)
        proj = (
            jnp.dot(residual, basis, precision=highest, preferred_element_type=jnp.float32)
            / feat_count
        )
        coef = lax.dot_general(proj, basis, (((1,), (1,)), ((), ())), precision=highest)
        solved = ridge_solve(factor, coef)
        back = jnp.dot(solved, basis, precision=highest, preferred_element_type=jnp.float32)
        local = weights + (proj - back) / ridge
        summed, primal_groups = lax.psum((local, primal_part), "frames")
        updated = penalty / (ridge_weight + penalty * group_count) * summed
        moved = updated - weights
        change, primal = lax.psum((jnp.sum(moved * moved), primal_groups), "feat")
        ratio = (primal / (total_frames * class_count) + epsilon) / (
            group_count * penalty * penalty * change / (total_features * class_count) + epsilon
        )
        next_penalty = penalty * jnp.sqrt(jnp.sqrt(ratio))
        duals = duals * (penalty / next_penalty)
        penalty = next_penalty
        weights = updated
    duals = lax.dynamic_slice_in_dim(duals, offset, share, 1)
    return (weights, duals, penalty)


def solution(mesh):
    return jax.shard_map(
        shards,
        mesh=mesh,
        in_specs=(
            P("frames", None),
            P(None, "feat"),
            P("feat"),
            P("frames"),
            P(None, "feat"),
            P(None, "frames"),
        ),
        out_specs=(P(None, "feat"), P(None, ("frames", "feat")), P()),
        check_vma=False,
    )
```

profile of v0, /device:TPU:0, one launch (start us, length us, event | category | flops | bytes accessed | tf_op | source)
XLA Modules:
  0.0 297.5 jit_solution(15187236382029461404)
XLA Ops:
  7.2 0.0 all-reduce.8.cloned.1.call-start
  7.2 1.4 copy-done
  8.7 13.2 %fusion.1 = f32[256,1024]{1,0:T(8,128)S(1)} fusion(f32[256,440]{0,1:T(8,128)} %param.10, f32[440,1024]{1,0:T(8,128)S(1)} %copy-done, f32[1024]{0:T(1024)} %param.12), kind=kOutput, calls=%fused_computation.4 | convolution fusion | flops 1384644608 | bytes 3305472 | tf_op jit(solution)/shard_map/dot_general | solution.py:14
  21.8 1.9 convolution_bitcast_fusion
  23.7 0.0 all-reduce.8.cloned.1.call-update
  23.7 0.2 all-reduce.10.cloned.1.call-start
  24.0 1.7 fusion.69
  25.7 1.8 copy.9
  27.5 1.1 fusion.10
  28.6 0.7 copy-done.8
  29.3 0.6 cholesky.115
  29.9 12.5 %cholesky.49 = f32[128,128]{1,0:T(8,128)S(1)} custom-call(f32[128,128]{1,0:T(8,128)} %cholesky.115), custom_call_target="Cholesky" | custom-call | tf_op jit(solution)/shard_map/jit(cholesky)/cholesky | solution.py:54
  42.5 0.6 select_reduce_fusion.1
  43.1 11.3 %custom-call.17 = f32[1,128,128]{1,2,0:T(8,128)} custom-call(f32[1,128,128]{2,1,0:T(8,128)} %get-tuple-element.63), custom_call_target="InvertDiagBlocksLowerTriangular" | custom-call | tf_op jit(solution)/shard_map/jit(cholesky)/cholesky | solution.py:54
  54.4 0.7 cholesky.111
  55.1 1.7 constant_dynamic-update-slice_fusion
  56.8 1.7 convolution_subtract_fusion.6
  58.5 12.5 %cholesky.103 = f32[128,128]{1,0:T(8,128)S(1)} custom-call(f32[128,128]{1,0:T(8,128)} %convolution_subtract_fusion.6), custom_call_target="Cholesky" | custom-call | tf_op jit(solution)/shard_map/jit(cholesky)/cholesky | solution.py:54
  71.1 0.6 select_reduce_fusion
  71.7 0.7 compare_reduce_fusion
  73.8 1.7 select_select_fusion
  75.5 0.1 broadcast.169
  75.5 7.0 %while.8 = (s32[]{:T(128)}, f32[256,256]{1,0:T(8,128)}, s32[2,2]{1,0:T(2,128)S(1)}, f32[2,128,128]{2,1,0:T(8,128)}, s32[]{:T(128)}) while((s32[]{:T(128)}, f32[256,256]{1,0:T(8,128)}, s32[2,2]{1,0:T(2,128)S(1)}, f32[2,128,128]{2,1,0:T(8,128)}, s32[]{:T(128)}) %tuple.44), condition=%wide.while_cond, body=%wide.while_body.sunk | while | flops 2 | bytes 132205 | solution.py:21
  75.5 0.6 fusion.100
  76.1 2.9 bitcast_dynamic-update-slice_fusion.2
  79.1 0.6 fusion.100
  79.6 2.9 bitcast_dynamic-update-slice_fusion.2
  82.5 21.1 %custom-call.20 = f32[2,128,128]{1,2,0:T(8,128)} custom-call(f32[2,128,128]{2,1,0:T(8,128)} %get-tuple-element.33), custom_call_target="InvertDiagBlocksLowerTriangular" | custom-call | tf_op jit(solution)/shard_map/triangular_solve/custom-call.0 | solution.py:21
  103.6 1.7 fusion.66
  105.3 1.9 convolution_multiply_fusion.1
  107.2 1.2 fusion.70
  108.5 0.3 fusion.33
  108.8 0.3 convolution_subtract_fusion.5
  109.1 0.3 fusion.47
  109.3 0.3 fusion.48
  109.6 0.3 convolution_subtract_fusion.4
  109.9 0.3 fusion.44
  110.2 1.6 fusion.3
  111.9 0.0 all-reduce.12.cloned.1.call-start
  111.9 1.6 multiply_reduce_fusion.3
  113.5 9.0 %psum.71 = f32[]{:T(128)} all-reduce(f32[]{:T(128)} %multiply_reduce_fusion.3), channel_id=1, replica_groups=mesh['frames'=4,'feat'=8] {'frames'}, use_global_device_ids=true, to_apply=%region_2.3 | all-reduce | flops 1 | bytes 8 | tf_op jit(solution)/shard_map/psum | solution.py:73
  122.5 26.2 %all-reduce.10.cloned.1.call-done = f32[147,1024]{1,0:T(8,128)} async-done(((f32[147,1024]{1,0:T(8,128)}), f32[147,1024]{1,0:T(8,128)}) %all-reduce.10.cloned.1.call-update) | async-done | bytes 602128 | tf_op jit(solution)/shard_map/psum | solution.py:73
  148.7 3.0 %fusion.6 = f32[147,256]{1,0:T(8,128)} fusion(f32[256,1024]{1,0:T(8,128)S(1)} %fusion.1, f32[147,1024]{1,0:T(8,128)} %all-reduce.10.cloned.1.call-done), kind=kOutput, calls=%fused_computation.21 | convolution fusion | flops 462572544 | bytes 1801216 | tf_op jit(solution)/shard_map/dot_general | solution.py:60
  151.7 0.0 all-reduce.14.cloned.1.call-start
  151.8 1.8 multiply_reduce_fusion.1
  153.6 22.0 %all-reduce.2 = (f32[]{:T(128)}, f32[]{:T(128)}) all-reduce(f32[]{:T(128)} %psum.71, f32[]{:T(128)} %multiply_reduce_fusion.1), channel_id=1, replica_groups=mesh['frames'=4,'feat'=8] {'feat'}, use_global_device_ids=true, to_apply=%region_3.4 | all-reduce | flops 2 | bytes 16 | tf_op jit(solution)/shard_map/psum | solution.py:76
  177.1 45.5 %all-reduce.12.cloned.1.call-done = f32[147,256]{1,0:T(8,128)} async-done(((f32[147,256]{1,0:T(8,128)}), f32[147,256]{1,0:T(8,128)}) %all-reduce.12.cloned.1.call-update) | async-done | bytes 150544 | tf_op jit(solution)/shard_map/psum | solution.py:61
  222.6 1.9 convolution_multiply_fusion
  224.4 1.2 fusion.71
  225.7 0.3 fusion.31
  226.0 0.3 convolution_subtract_fusion.3
  226.3 0.3 fusion.45
  226.6 0.3 fusion.46
  226.9 0.3 convolution_subtract_fusion.2
  227.1 0.3 fusion.43
  227.4 1.6 fusion.5
  229.1 1.1 fusion.54
  230.2 0.7 multiply_reduce_fusion.2
  230.9 6.3 %psum.77 = f32[]{:T(128)} all-reduce(f32[]{:T(128)} %multiply_reduce_fusion.2), channel_id=1, replica_groups=mesh['frames'=4,'feat'=8] {'frames'}, use_global_device_ids=true, to_apply=%region_14.17 | all-reduce | flops 1 | bytes 8 | tf_op jit(solution)/shard_map/psum | solution.py:73
  237.2 25.8 %all-reduce.14.cloned.1.call-done = f32[147,1024]{1,0:T(8,128)} async-done(((f32[147,1024]{1,0:T(8,128)}), f32[147,1024]{1,0:T(8,128)}) %all-reduce.14.cloned.1.call-update) | async-done | bytes 602128 | tf_op jit(solution)/shard_map/psum | solution.py:73
  263.0 2.6 multiply_reduce_fusion
  265.6 22.0 %all-reduce.1 = (f32[]{:T(128)}, f32[]{:T(128)}) all-reduce(f32[]{:T(128)} %psum.77, f32[]{:T(128)} %get-tuple-element.52), channel_id=1, replica_groups=mesh['frames'=4,'feat'=8] {'feat'}, use_global_device_ids=true, to_apply=%region_15.18 | all-reduce | flops 2 | bytes 16 | tf_op jit(solution)/shard_map/psum | solution.py:76
  289.1 0.1 dynamic-slice_multiply_fusion
  289.2 0.7 copy.10
  (26 shorter events, 0.1 us)
Async XLA Ops:
  7.2 1.5 copy-start
  7.2 14.7 %copy-start.2 = (f32[147,1024]{1,0:T(8,128)S(1)}, f32[147,1024]{1,0:T(8,128)}, u32[]{:S(2)}) copy-start(f32[147,1024]{1,0:T(8,128)} %param.14) | copy-start | bytes 1806340
  7.2 96.4 %all-reduce.8.cloned.1.call-start = ((), (), s32[]{:S(2)}) async-start(), calls=%async_computation | async-start | bytes 311296 | tf_op jit(solution)/shard_map/psum | solution.py:61
  23.7 124.9 %all-reduce.10.cloned.1.call-start = ((), (), s32[]{:S(2)}) async-start(), calls=%async_computation.1 | async-start | bytes 1245184 | tf_op jit(solution)/shard_map/psum | solution.py:73
  27.5 76.1 %copy-start.9 = (s32[256]{0:T(256)S(1)}, s32[256]{0:T(256)}, u32[]{:S(2)}) copy-start(s32[256]{0:T(256)} %param.13) | copy-start | bytes 3076
  28.6 0.7 copy-start.8
  105.3 3.1 %copy-start.5 = (f32[147,256]{1,0:T(8,128)}, f32[147,256]{1,0:T(8,128)S(1)}, u32[]{:S(2)}) copy-start(f32[147,256]{1,0:T(8,128)S(1)} %get-tuple-element.54) | copy-start | bytes 451588
  105.3 3.1 %copy-start.6 = (f32[2,128,128]{1,2,0:T(8,128)S(1)}, f32[2,128,128]{1,2,0:T(8,128)}, u32[]{:S(2)}) copy-start(f32[2,128,128]{1,2,0:T(8,128)} %custom-call.20) | copy-start | bytes 393220
  105.3 3.4 %copy-start.3 = (f32[256,256]{1,0:T(8,128)S(1)}, f32[256,256]{1,0:T(8,128)}, u32[]{:S(2)}) copy-start(f32[256,256]{1,0:T(8,128)} %get-tuple-element.117) | copy-start | bytes 786436
  111.9 110.7 %all-reduce.12.cloned.1.call-start = ((), (), s32[]{:S(2)}) async-start(), calls=%async_computation.2 | async-start | bytes 311296 | tf_op jit(solution)/shard_map/psum | solution.py:61
  148.7 3.1 %copy-start.1 = (f32[147,1024]{1,0:T(8,128)S(1)}, f32[147,1024]{1,0:T(8,128)}, u32[]{:S(2)}) copy-start(f32[147,1024]{1,0:T(8,128)} %all-reduce.10.cloned.1.call-done) | copy-start | bytes 1806340
  151.7 111.3 %all-reduce.14.cloned.1.call-start = ((), (), s32[]{:S(2)}) async-start(), calls=%async_computation.3 | async-start | bytes 1245184 | tf_op jit(solution)/shard_map/psum | solution.py:73
  222.6 3.1 %copy-start.7 = (f32[2,128,128]{1,2,0:T(8,128)S(1)}, f32[2,128,128]{1,2,0:T(8,128)}, u32[]{:S(2)}) copy-start(f32[2,128,128]{1,2,0:T(8,128)} %custom-call.20) | copy-start | bytes 393220
  222.6 3.4 %copy-start.4 = (f32[256,256]{1,0:T(8,128)S(1)}, f32[256,256]{1,0:T(8,128)}, u32[]{:S(2)}) copy-start(f32[256,256]{1,0:T(8,128)} %get-tuple-element.117) | copy-start | bytes 786436
Sparse Core Ops, SparseCore 0:
  23.9 73.2 all-reduce.7
  112.0 36.6 all-reduce.9
  152.6 69.9 all-reduce.11
  229.2 33.7 all-reduce.13
where the time goes:
time: 299 us; the launch traced here: 298 us
  waiting for transfers between devices  97.5 us (33%)
  other arithmetic  71.9 us (24%)
  blocking collectives  59.2 us (20%)
  matrix products  36.1 us (12%)
  between operations  19.5 us (7%)
  local copies, waits for them, and re-layouts  13 us (4%)
    psum x2, waiting for transfers between devices, shards(): summed, primal_groups = lax.psum((local, primal_part), 'frames')  51.9 us
    psum x2, waiting for transfers between devices, shards(): predicted = lax.psum(partial_value, 'feat')  45.5 us
    psum x2, blocking collectives, shards(): change, primal = lax.psum((jnp.sum(moved * moved), primal_groups), 'feat')  44 us
    another operation x6, other arithmetic, shards(): factor = jnp.linalg.cholesky(inner_matrix)  38.4 us
    another operation x4, other arithmetic, ridge_solve(): lax.linalg.triangular_solve(factor, right, left_side=False, lower=True, t...  22.8 us
    psum x2, blocking collectives, shards(): summed, primal_groups = lax.psum((local, primal_part), 'frames')  15.3 us
    dot_general x1, matrix products, cosine_features(): jnp.dot(acoustic, projection, precision=highest, preferred_element_type=j...  13.2 us
    another operation x7, local copies, waits for them, and re-layouts, ridge_solve(): lax.linalg.triangular_solve(factor, right, left_side=False, lower=True, t...  7.03 us
  transfers between devices with their start and end apart: 4, of which 3 were waited for; matrix products, arithmetic and copies ran while one was open for 28% of the time, Pallas kernels for 0%

commit v1 on v0

--- a/solution.py
+++ b/solution.py
@@ -58,7 +58,8 @@
     penalty = jnp.ones((), jnp.float32)
     for iteration in range(ITERS):
         partial_value = lax.dot_general(weights, basis, (((1,), (1,)), ((), ())), precision=highest)
-        predicted = lax.psum(partial_value, "feat")
+        parts = lax.all_gather(partial_value, "feat", axis=0, tiled=False)
+        predicted = parts.sum(axis=0)
         miss, duals, residual = proximal(predicted, duals, target, penalty)
         mine = lax.dynamic_slice_in_dim(miss, offset, share, 1)
         primal_part = jnp.sum(mine * mine)

time: 299 us -> 272 us (0.910)
  waiting for transfers between devices: 97.5 us -> 69.6 us
  other arithmetic: 71.9 us -> 75.9 us
    psum x2 -> x0, waiting for transfers between devices: 45.5 us -> none  [shards(): predicted = lax.psum(partial_value, 'feat')]
    psum x2, waiting for transfers between devices: 51.9 us -> 61.3 us  [shards(): summed, primal_groups = lax.psum((local, primal_part), 'frames')]
    all_gather x0 -> x2, waiting for transfers between devices: none -> 8.18 us  [shards(): parts = lax.all_gather(partial_value, 'feat', axis=0, tiled=False)]
    reduce_sum x0 -> x2, other arithmetic: none -> 4.08 us  [shards(): predicted = parts.sum(axis=0)]
  transfers between devices with their start and end apart: 4 -> 4, of which waited for: 3 -> 3; matrix products, arithmetic and copies ran while one was open for 28% -> 31% of each run, Pallas kernels for 0% -> 0%
where the time goes in v1:
time: 272 us; the launch traced here: 271 us
  other arithmetic  75.9 us (28%)
  waiting for transfers between devices  69.6 us (26%)
  blocking collectives  56.9 us (21%)
  matrix products  36.1 us (13%)
  between operations  19.3 us (7%)
  local copies, waits for them, and re-layouts  13 us (5%)
    psum x2, waiting for transfers between devices, shards(): summed, primal_groups = lax.psum((local, primal_part), 'frames')  61.3 us
    psum x2, blocking collectives, shards(): change, primal = lax.psum((jnp.sum(moved * moved), primal_groups), 'feat')  44.2 us
    another operation x6, other arithmetic, shards(): factor = jnp.linalg.cholesky(inner_matrix)  38.3 us
    another operation x4, other arithmetic, ridge_solve(): lax.linalg.triangular_solve(factor, right, left_side=False, lower=True, t...  22.8 us
    dot_general x1, matrix products, cosine_features(): jnp.dot(acoustic, projection, precision=highest, preferred_element_type=j...  13.2 us
    psum x2, blocking collectives, shards(): summed, primal_groups = lax.psum((local, primal_part), 'frames')  12.8 us
    all_gather x2, waiting for transfers between devices, shards(): parts = lax.all_gather(partial_value, 'feat', axis=0, tiled=False)  8.18 us
    another operation x7, local copies, waits for them, and re-layouts, ridge_solve(): lax.linalg.triangular_solve(factor, right, left_side=False, lower=True, t...  7.02 us
  transfers between devices with their start and end apart: 4, of which 3 were waited for; matrix products, arithmetic and copies ran while one was open for 31% of the time, Pallas kernels for 0%

profile of v1, /device:TPU:0, one launch (start us, length us, event | category | flops | bytes accessed | tf_op | source)
XLA Modules:
  0.0 271.2 jit_solution(11781592948618252944)
XLA Ops:
  7.2 1.4 copy-done
  8.7 13.2 %fusion.1 = f32[256,1024]{1,0:T(8,128)S(1)} fusion(f32[256,440]{0,1:T(8,128)} %param.10, f32[440,1024]{1,0:T(8,128)S(1)} %copy-done, f32[1024]{0:T(1024)} %param.12), kind=kOutput, calls=%fused_computation.4 | convolution fusion | flops 1384644608 | bytes 3305472 | tf_op jit(solution)/shard_map/dot_general | solution.py:14
  21.8 1.9 convolution_bitcast_fusion.1
  23.7 0.2 all-reduce.6.cloned.1.call-start
  24.0 1.7 fusion.68
  25.7 1.8 copy.12
  27.5 1.1 fusion.9
  28.6 0.7 copy-done.8
  29.3 0.6 cholesky.115
  29.9 12.6 %cholesky.49 = f32[128,128]{1,0:T(8,128)S(1)} custom-call(f32[128,128]{1,0:T(8,128)} %cholesky.115), custom_call_target="Cholesky" | custom-call | tf_op jit(solution)/shard_map/jit(cholesky)/cholesky | solution.py:54
  42.5 0.6 select_reduce_fusion.1
  43.1 11.3 %custom-call.17 = f32[1,128,128]{1,2,0:T(8,128)} custom-call(f32[1,128,128]{2,1,0:T(8,128)} %get-tuple-element.63), custom_call_target="InvertDiagBlocksLowerTriangular" | custom-call | tf_op jit(solution)/shard_map/jit(cholesky)/cholesky | solution.py:54
  54.4 0.7 cholesky.111
  55.1 1.7 constant_dynamic-update-slice_fusion
  56.8 1.7 convolution_subtract_fusion.6
  58.6 12.5 %cholesky.103 = f32[128,128]{1,0:T(8,128)S(1)} custom-call(f32[128,128]{1,0:T(8,128)} %convolution_subtract_fusion.6), custom_call_target="Cholesky" | custom-call | tf_op jit(solution)/shard_map/jit(cholesky)/cholesky | solution.py:54
  71.1 0.6 select_reduce_fusion
  71.7 0.6 compare_reduce_fusion
  73.6 1.7 select_select_fusion
  75.3 0.1 broadcast.169
  75.4 7.0 %while.8 = (s32[]{:T(128)}, f32[256,256]{1,0:T(8,128)}, s32[2,2]{1,0:T(2,128)S(1)}, f32[2,128,128]{2,1,0:T(8,128)}, s32[]{:T(128)}) while((s32[]{:T(128)}, f32[256,256]{1,0:T(8,128)}, s32[2,2]{1,0:T(2,128)S(1)}, f32[2,128,128]{2,1,0:T(8,128)}, s32[]{:T(128)}) %tuple.44), condition=%wide.while_cond, body=%wide.while_body.sunk | while | flops 2 | bytes 132205 | solution.py:21
  75.4 0.6 fusion.99
  76.0 2.9 %bitcast_dynamic-update-slice_fusion.2 = f32[2,128,128]{2,1,0:T(8,128)} fusion(f32[2,128,128]{2,1,0:T(8,128)} %get-tuple-element.105, s32[]{:T(128)S(6)} %copy.19, f32[256,256]{1,0:T(8,128)} %get-tuple-element.108, s32[]{:T(128)} %bitcast.87, s32[]{:T(128)} %bitcast.88), kind=kLoop, calls=%fused_computation.clone.1 | loop fusion | bytes 132100 | tf_op jit(solution)/shard_map/triangular_solve | solution.py:21
  78.9 0.6 fusion.99
  79.5 2.8 %bitcast_dynamic-update-slice_fusion.2 = f32[2,128,128]{2,1,0:T(8,128)} fusion(f32[2,128,128]{2,1,0:T(8,128)} %get-tuple-element.105, s32[]{:T(128)S(6)} %copy.19, f32[256,256]{1,0:T(8,128)} %get-tuple-element.108, s32[]{:T(128)} %bitcast.87, s32[]{:T(128)} %bitcast.88), kind=kLoop, calls=%fused_computation.clone.1 | loop fusion | bytes 132100 | tf_op jit(solution)/shard_map/triangular_solve | solution.py:21
  82.3 21.1 %custom-call.20 = f32[2,128,128]{1,2,0:T(8,128)} custom-call(f32[2,128,128]{2,1,0:T(8,128)} %get-tuple-element.33), custom_call_target="InvertDiagBlocksLowerTriangular" | custom-call | tf_op jit(solution)/shard_map/triangular_solve/custom-call.0 | solution.py:21
  103.4 2.0 reduce_sum.54
  105.5 1.7 fusion.65
  107.2 1.9 convolution_multiply_fusion.1
  109.1 1.2 fusion.69
  110.3 0.3 fusion.32
  110.6 0.3 convolution_subtract_fusion.5
  110.9 0.3 fusion.46
  111.2 0.3 fusion.47
  111.5 0.3 convolution_subtract_fusion.4
  111.8 0.3 fusion.43
  112.1 1.6 fusion.3
  113.7 0.0 all-gather.9.cloned.1.call-start
  113.8 36.7 %all-reduce.6.cloned.1.call-done = f32[147,1024]{1,0:T(8,128)} async-done(((f32[147,1024]{1,0:T(8,128)}), f32[147,1024]{1,0:T(8,128)}) %all-reduce.6.cloned.1.call-update) | async-done | bytes 602128 | tf_op jit(solution)/shard_map/psum | solution.py:74
  150.5 3.0 %convolution_bitcast_fusion = f32[1,147,256]{2,1,0:T(8,128)} fusion(f32[256,1024]{1,0:T(8,128)S(1)} %fusion.1, f32[147,1024]{1,0:T(8,128)} %all-reduce.6.cloned.1.call-done), kind=kOutput, calls=%fused_computation.13 | convolution fusion | flops 462572544 | bytes 1801216 | tf_op jit(solution)/shard_map/dot_general | solution.py:60
  153.5 0.0 all-reduce.8.cloned.1.call-start
  153.6 1.6 multiply_reduce_fusion.3
  155.2 6.4 %psum.56 = f32[]{:T(128)} all-reduce(f32[]{:T(128)} %multiply_reduce_fusion.3), channel_id=1, replica_groups=mesh['frames'=4,'feat'=8] {'frames'}, use_global_device_ids=true, to_apply=%region_2.3 | all-reduce | flops 1 | bytes 8 | tf_op jit(solution)/shard_map/psum | solution.py:74
  161.5 1.9 multiply_reduce_fusion.1
  163.4 22.2 %all-reduce.2 = (f32[]{:T(128)}, f32[]{:T(128)}) all-reduce(f32[]{:T(128)} %psum.56, f32[]{:T(128)} %multiply_reduce_fusion.1), channel_id=1, replica_groups=mesh['frames'=4,'feat'=8] {'feat'}, use_global_device_ids=true, to_apply=%region_3.4 | all-reduce | flops 2 | bytes 16 | tf_op jit(solution)/shard_map/psum | solution.py:77
  187.1 8.2 %all-gather.9.cloned.1.call-done = f32[8,147,256]{2,1,0:T(8,128)} async-done(((f32[1,147,256]{2,1,0:T(8,128)}), f32[8,147,256]{2,1,0:T(8,128)}) %all-gather.9.cloned.1.call-update) | async-done | bytes 1204240 | tf_op jit(solution)/shard_map/all_gather | solution.py:61
  195.2 2.0 reduce_sum.57
  197.3 1.9 convolution_multiply_fusion
  199.2 1.2 fusion.70
  200.4 0.3 fusion.30
  200.7 0.3 convolution_subtract_fusion.3
  201.0 0.3 fusion.44
  201.3 0.3 fusion.45
  201.6 0.3 convolution_subtract_fusion.2
  201.9 0.3 fusion.42
  202.2 1.6 fusion.5
  203.9 1.1 fusion.53
  204.9 0.7 multiply_reduce_fusion.2
  205.7 6.4 %psum.61 = f32[]{:T(128)} all-reduce(f32[]{:T(128)} %multiply_reduce_fusion.2), channel_id=1, replica_groups=mesh['frames'=4,'feat'=8] {'frames'}, use_global_device_ids=true, to_apply=%region_14.17 | all-reduce | flops 1 | bytes 8 | tf_op jit(solution)/shard_map/psum | solution.py:74
  212.1 24.6 %all-reduce.8.cloned.1.call-done = f32[147,1024]{1,0:T(8,128)} async-done(((f32[147,1024]{1,0:T(8,128)}), f32[147,1024]{1,0:T(8,128)}) %all-reduce.8.cloned.1.call-update) | async-done | bytes 602128 | tf_op jit(solution)/shard_map/psum | solution.py:74
  236.7 2.6 multiply_reduce_fusion
  239.3 22.0 %all-reduce.1 = (f32[]{:T(128)}, f32[]{:T(128)}) all-reduce(f32[]{:T(128)} %psum.61, f32[]{:T(128)} %get-tuple-element.52), channel_id=1, replica_groups=mesh['frames'=4,'feat'=8] {'feat'}, use_global_device_ids=true, to_apply=%region_15.18 | all-reduce | flops 2 | bytes 16 | tf_op jit(solution)/shard_map/psum | solution.py:77
  262.8 0.1 dynamic-slice_multiply_fusion
  262.9 0.7 copy.13
  (28 shorter events, 0.2 us)
Async XLA Ops:
  7.2 1.5 copy-start
  7.2 14.7 %copy-start.2 = (f32[147,1024]{1,0:T(8,128)S(1)}, f32[147,1024]{1,0:T(8,128)}, u32[]{:S(2)}) copy-start(f32[147,1024]{1,0:T(8,128)} %param.14) | copy-start | bytes 1806340
  7.2 96.2 %all-gather.7.cloned.1.call-start = ((), (), s32[]{:S(2)}) async-start(), calls=%async_computation.2 | async-start | bytes 1400832 | tf_op jit(solution)/shard_map/all_gather | solution.py:61
  23.7 126.8 %all-reduce.6.cloned.1.call-start = ((), (), s32[]{:S(2)}) async-start(), calls=%async_computation | async-start | bytes 1245184 | tf_op jit(solution)/shard_map/psum | solution.py:74
  28.6 0.7 copy-start.8
  55.1 50.4 %copy-start.9 = (s32[256]{0:T(256)S(1)}, s32[256]{0:T(256)}, u32[]{:S(2)}) copy-start(s32[256]{0:T(256)} %param.13) | copy-start | bytes 3076
  107.2 3.1 %copy-start.5 = (f32[147,256]{1,0:T(8,128)}, f32[147,256]{1,0:T(8,128)S(1)}, u32[]{:S(2)}) copy-start(f32[147,256]{1,0:T(8,128)S(1)} %get-tuple-element.54) | copy-start | bytes 451588
  107.2 3.1 %copy-start.6 = (f32[2,128,128]{1,2,0:T(8,128)S(1)}, f32[2,128,128]{1,2,0:T(8,128)}, u32[]{:S(2)}) copy-start(f32[2,128,128]{1,2,0:T(8,128)} %custom-call.20) | copy-start | bytes 393220
  107.2 3.4 %copy-start.3 = (f32[256,256]{1,0:T(8,128)S(1)}, f32[256,256]{1,0:T(8,128)}, u32[]{:S(2)}) copy-start(f32[256,256]{1,0:T(8,128)} %get-tuple-element.117) | copy-start | bytes 786436
  113.7 81.5 %all-gather.9.cloned.1.call-start = ((), (), s32[]{:S(2)}) async-start(), calls=%async_computation.3 | async-start | bytes 1400832 | tf_op jit(solution)/shard_map/all_gather | solution.py:61
  150.5 11.1 %copy-start.1 = (f32[147,1024]{1,0:T(8,128)S(1)}, f32[147,1024]{1,0:T(8,128)}, u32[]{:S(2)}) copy-start(f32[147,1024]{1,0:T(8,128)} %all-reduce.6.cloned.1.call-done) | copy-start | bytes 1806340
  153.5 83.2 %all-reduce.8.cloned.1.call-start = ((), (), s32[]{:S(2)}) async-start(), calls=%async_computation.1 | async-start | bytes 1245184 | tf_op jit(solution)/shard_map/psum | solution.py:74
  197.3 3.1 %copy-start.7 = (f32[2,128,128]{1,2,0:T(8,128)S(1)}, f32[2,128,128]{1,2,0:T(8,128)}, u32[]{:S(2)}) copy-start(f32[2,128,128]{1,2,0:T(8,128)} %custom-call.20) | copy-start | bytes 393220
  197.3 3.4 %copy-start.4 = (f32[256,256]{1,0:T(8,128)S(1)}, f32[256,256]{1,0:T(8,128)}, u32[]{:S(2)}) copy-start(f32[256,256]{1,0:T(8,128)} %get-tuple-element.117) | copy-start | bytes 786436
Sparse Core Ops, SparseCore 0:
  23.8 45.1 all-gather.6
  113.8 36.5 all-reduce.5
  153.7 41.5 all-gather.8
  204.0 32.6 all-reduce.7
